TPU v7x, 128 devices: a whole 4x4x4 slice. The times are simulated.
128 devices in a mesh: dp: 8 (over z, core), expert: 16 (over y, x).
Axes of the slice: x: 4, y: 4, z: 4, core: 2. Of those that a mesh axis runs over, the one named last changes fastest.
Arguments:
- inputs: bfloat16 [16384, 2048], P(('dp', 'expert')), may hold values from -6 to 6
- out_grad: bfloat16 [16384, 2048], P(('dp', 'expert')), may hold values from -6 to 6
- combine: float32 [16384, 8], P(('dp', 'expert')), may hold values from 0 to 1, as said below
- routes: int32 [16384, 8], P(('dp', 'expert')), may hold values from 0 to 63, all different within a row; in each aligned block of 128 rows (0 to 127, 128 to 255, ...) at most 24 rows name the same one
- saved_hidden: bfloat16 [8, 64, 16, 24, 768], P('dp', 'expert'), may hold values from -6 to 6
- down_weight: bfloat16 [64, 2048, 768], P('expert'), may hold values from -0.21875 to 0.21875
- router_weight: bfloat16 [64, 2048], replicated, may hold values from -0.125 to 0.125
Outputs:
- hidden_grad: bfloat16 [8, 64, 16, 24, 768], P('dp', 'expert')
- down_grad: bfloat16 [64, 2048, 768], P('expert', 'dp')
- input_grad: bfloat16 [16384, 2048], P(('dp', 'expert'))
- router_grad: float32 [64, 2048], replicated
Inputs may be any that keep to these rules, and one draw needn't show every extreme that they name: `routes`: each token names 8 different experts; among the 128 tokens of one device no expert is named by more than 24 tokens, a bound that some block reaches. `combine`: each token's 8 weights are positive and sum to one.
All inputs are finite; a program needn't handle non-finite values.
Results may differ from a plain program's by a relative error of at most 0.017.
Values may be sent and summed in bfloat16 or wider, within the bound.
A program may use at most 128 MiB of HBM per device.

v0:
```python
import jax
import jax.numpy as jnp
from jax import lax
from jax.sharding import PartitionSpec as P


def make_marks(block_routes, total_experts):
    return block_routes[:, :, None] == jnp.arange(total_experts, dtype=jnp.int32)[None, None, :]


def slot_positions(route_marks):
    counts = jnp.sum(route_marks.astype(jnp.bfloat16), axis=1)
    token_order = jnp.arange(route_marks.shape[0], dtype=jnp.int32)
    earlier = (token_order[None, :] < token_order[:, None]).astype(jnp.bfloat16)
    before = jnp.dot(earlier, counts, preferred_element_type=jnp.float32)
    picked = jnp.sum(jnp.where(route_marks, before[:, None, :], 0.0), axis=2)
    return picked.astype(jnp.int32)


def pack_rows(scaled, lane_index, owner_slot, positions, local_experts, groups, capacity):
    width = scaled.shape[-1]
    flat_index = (owner_slot * groups + lane_index) * capacity + positions
    zero_rows = jnp.zeros((local_experts * groups * capacity, width), jnp.bfloat16)
    filled = zero_rows.at[flat_index.reshape(-1)].set(scaled.reshape(-1, width))
    return filled.reshape(local_experts, groups, capacity, width)


def local(inputs, out_grad, combine, routes, saved_hidden, down_weight, router_weight):
    token_count, width = out_grad.shape
    local_experts = down_weight.shape[0]
    total_experts = router_weight.shape[0]
    groups = lax.axis_size("expert")
    capacity = saved_hidden.shape[3]
    hidden_width = saved_hidden.shape[4]
    route_marks = make_marks(routes, total_experts)
    positions = slot_positions(route_marks)
    owner_dev = routes // local_experts
    owner_slot = routes % local_experts
    scaled = (combine[:, :, None] * out_grad[:, None, :].astype(jnp.float32)).astype(jnp.bfloat16)
    packed = pack_rows(scaled, owner_dev, owner_slot, positions, local_experts, groups, capacity)
    received = lax.all_to_all(packed, "expert", split_axis=1, concat_axis=1, tiled=True)
    hidden_local = saved_hidden[0]
    products_list = []
    hidden_list = []
    weight_terms = []
    for expert in range(local_experts):
        slot_rows = received[expert].reshape(groups * capacity, width)
        slot_acts = hidden_local[expert].reshape(groups * capacity, hidden_width)
        weight = down_weight[expert]
        recomputed = lax.dot_general(
            slot_acts, weight, (((1,), (1,)), ((), ())), preferred_element_type=jnp.float32
        )
        products_list.append(jnp.sum(recomputed * slot_rows.astype(jnp.float32), axis=1))
        hidden_list.append(
            jnp.dot(slot_rows, weight, preferred_element_type=jnp.float32).astype(jnp.bfloat16)
        )
        weight_terms.append(
            lax.dot_general(
                slot_rows, slot_acts, (((0,), (0,)), ((), ())), preferred_element_type=jnp.float32
            )
        )
    down_grad = lax.psum_scatter(
        jnp.stack(weight_terms).astype(jnp.bfloat16), "dp", scatter_dimension=1, tiled=True
    )
    hidden_grad = jnp.stack(hidden_list).reshape(1, local_experts, groups, capacity, hidden_width)
    slot_products = jnp.stack(products_list).reshape(local_experts, groups, capacity)
    returned = lax.all_to_all(slot_products, "expert", split_axis=1, concat_axis=1, tiled=True)
    pair_index = (owner_slot * groups + owner_dev) * capacity + positions
    pair_sums = returned.reshape(-1)[pair_index]
    logit_grad = pair_sums - combine * jnp.sum(pair_sums, axis=1, keepdims=True)
    dense_grad = jnp.sum(jnp.where(route_marks, logit_grad[:, :, None], 0.0), axis=1).astype(
        jnp.bfloat16
    )
    input_grad = jnp.dot(dense_grad, router_weight, preferred_element_type=jnp.float32).astype(
        jnp.bfloat16
    )
    router_part = lax.dot_general(
        dense_grad, inputs, (((0,), (0,)), ((), ())), preferred_element_type=jnp.float32
    )
    router_grad = lax.psum(router_part, ("dp", "expert"))
    return (hidden_grad, down_grad, input_grad, router_grad)


def solution(mesh):
    placed = (
        P(("dp", "expert"), None),
        P(("dp", "expert"), None),
        P(("dp", "expert"), None),
        P(("dp", "expert"), None),
        P("dp", "expert", None, None, None),
        P("expert", None, None),
        P(),
    )
    return jax.shard_map(
        local,
        mesh=mesh,
        in_specs=placed,
        out_specs=(
            P("dp", "expert", None, None, None),
            P("expert", "dp", None),
            P(("dp", "expert"), None),
            P(),
        ),
        check_vma=False,
    )
```

profile of v0, /device:TPU:1, one launch (start us, length us, event | category | flops | bytes accessed | tf_op | source)
XLA Modules:
  0.0 366.2 jit_solution(16921963926218966697)
XLA Ops:
  8.0 0.8 fusion.55
  8.9 0.7 select_reduce_fusion.1
  9.7 0.7 compare_select_fusion.1
  10.6 0.8 copy.46
  11.5 1.1 convert_element_type.50
  12.6 10.6 %scatter_custom_fusion = bf16[1536,2048]{1,0:T(8,128)(2,1)} fusion(s32[1024]{0:T(1024)S(1)} %bitcast.110, f32[128,2048]{1,0:T(8,128)S(1)} %convert_element_type.50, f32[1024]{0:T(1024)S(1)} %mul.48, bf16[]{:T(256)} %constant.31.clone.1), kind=kCustom, calls=%fused_computation.5 | custom fusion | flops 4194304 | bytes 7344130 | tf_op jit(solution)/shard_map/scatter | solution.py:24
  23.2 6.6 %copy.47 = bf16[4,16,24,2048]{3,2,0,1:T(8,128)(2,1)} copy(bf16[4,16,24,2048]{3,2,1,0:T(8,128)(2,1)} %bitcast.85) | data formatting | bytes 12582912 | tf_op jit(solution)/shard_map/reshape | solution.py:25
  29.8 7.8 %all-to-all-start = ((bf16[4,16,24,2048]{3,2,0,1:T(8,128)(2,1)}), bf16[4,16,24,2048]{3,2,0,1:T(8,128)(2,1)}, u32[]{:S(2)}, u32[]{:S(2)}) async-start(bf16[4,16,24,2048]{3,2,0,1:T(8,128)(2,1)} %copy.47), calls=%async_computation | async-start | bytes 12582912 | tf_op jit(solution)/shard_map/all_to_all | solution.py:41
  37.8 1.2 fusion.70
  39.0 90.8 %all-to-all-done = bf16[4,16,24,2048]{3,2,0,1:T(8,128)(2,1)} async-done(((bf16[4,16,24,2048]{3,2,0,1:T(8,128)(2,1)}), bf16[4,16,24,2048]{3,2,0,1:T(8,128)(2,1)}, u32[]{:S(2)}, u32[]{:S(2)}) %all-to-all-start) | async-done | bytes 6291488 | tf_op jit(solution)/shard_map/all_to_all | solution.py:41
  129.9 4.8 %fusion.69 = (bf16[1,16,24,2048]{3,2,0,1:T(8,128)(2,1)S(1)}, bf16[1,16,24,2048]{3,2,0,1:T(8,128)(2,1)}, bf16[1,16,24,2048]{3,2,0,1:T(8,128)(2,1)S(1)}, bf16[1,16,24,2048]{3,2,0,1:T(8,128)(2,1)S(1)}) fusion(bf16[4,16,24,2048]{3,2,0,1:T(8,128)(2,1)} %all-to-all-done), kind=kLoop, calls=%fused_computation.80 | loop fusion | bytes 12582912 | tf_op jit(solution)/shard_map/slice | solution.py:47
  134.7 3.5 fusion.23
  138.2 3.6 multiply_reduce_fusion.2
  141.9 1.5 multiply_reduce_fusion.1
  143.4 3.5 fusion.24
  146.9 1.5 multiply_reduce_fusion.3
  148.4 3.5 fusion.22
  152.2 3.9 %multiply_reduce_fusion = f32[384]{0:T(512)S(1)} fusion(bf16[384,2048]{1,0:T(8,128)(2,1)} %bitcast.95, bf16[384,768]{1,0:T(8,128)(2,1)S(1)} %bitcast.98, bf16[4,2048,768]{2,1,0:T(8,128)(2,1)} %param.12), kind=kOutput, calls=%fused_computation.28 | convolution fusion | flops 1210318464 | bytes 5309952 | tf_op jit(solution)/shard_map/dot_general | solution.py:50
  156.9 5.4 %all-to-all-start.1 = ((f32[4,16,24]{2,0,1:T(4,128)}), f32[4,16,24]{2,0,1:T(4,128)S(1)}, u32[]{:S(2)}, u32[]{:S(2)}) async-start(f32[4,16,24]{2,0,1:T(4,128)} %pad_maximum_fusion.2), calls=%async_computation.2 | async-start | bytes 65536 | tf_op jit(solution)/shard_map/all_to_all | solution.py:67
  162.6 4.9 %fusion.25 = bf16[1,2048,768]{2,1,0:T(8,128)(2,1)} fusion(bf16[384,2048]{1,0:T(8,128)(2,1)} %bitcast.96, bf16[384,768]{1,0:T(8,128)(2,1)S(1)} %bitcast.99), kind=kOutput, calls=%fused_computation.36 | convolution fusion | flops 1209532416 | bytes 5308416 | tf_op jit(solution)/shard_map/dot_general | solution.py:58
  167.5 1.3 all-to-all-done.1
  168.8 6.2 %gather_fusion = f32[1024]{0:T(1024)S(1)} fusion(f32[1536]{0:T(1024)S(1)} %reshape.84, s32[1024]{0:T(1024)S(1)} %broadcast_clamp_fusion), kind=kCustom, calls=%fused_computation | custom fusion | bytes 12288 | tf_op jit(solution)/shard_map/gather | solution.py:69
  175.4 1.0 fusion.71
  176.5 10.7 %pad_maximum_fusion = bf16[4,2048,768]{2,1,0:T(8,128)(2,1)} fusion(bf16[1,2048,768]{2,1,0:T(8,128)(2,1)} %fusion.25, bf16[1,2048,768]{2,1,0:T(8,128)(2,1)} %fusion.24, bf16[1,2048,768]{2,1,0:T(8,128)(2,1)} %fusion.23, bf16[1,2048,768]{2,1,0:T(8,128)(2,1)} %fusion.22), kind=kLoop, calls=%fused_computation.2 | loop fusion | flops 18874368 | bytes 25165824 | tf_op jit(solution)/shard_map/stack | solution.py:63
  187.2 3.9 %fusion.51 = bf16[384,768]{1,0:T(8,128)(2,1)S(1)} fusion(bf16[384,2048]{1,0:T(8,128)(2,1)} %bitcast.97, bf16[4,2048,768]{2,1,0:T(8,128)(2,1)} %param.12), kind=kOutput, calls=%fused_computation.50 | convolution fusion | flops 1208254464 | bytes 5308416 | tf_op jit(solution)/shard_map/dot_general | solution.py:55
  191.1 3.4 fusion.42
  194.6 3.3 fusion.48
  197.9 4.1 %fusion.45 = bf16[384,768]{1,0:T(8,128)(2,1)S(1)} fusion(bf16[384,2048]{1,0:T(8,128)(2,1)S(1)} %bitcast.88, bf16[4,2048,768]{2,1,0:T(8,128)(2,1)} %param.12), kind=kOutput, calls=%fused_computation.48 | convolution fusion | flops 1208254464 | bytes 5308416 | tf_op jit(solution)/shard_map/dot_general | solution.py:55
  202.0 1.7 pad_maximum_fusion.1
  203.7 1.1 convolution_convert_fusion.4
  204.9 152.0 %all-reduce.2.cloned.1.call-done = f32[64,2048]{1,0:T(8,128)} async-done(((f32[64,2048]{1,0:T(8,128)}), f32[64,2048]{1,0:T(8,128)}) %all-reduce.2.cloned.1.call-update) | async-done | bytes 524304 | tf_op jit(solution)/shard_map/psum | solution.py:80
  356.9 1.9 copy.52
  (56 shorter events, 2.5 us)
Async XLA Ops:
  8.0 167.4 %copy-start = (bf16[128,2048]{1,0:T(8,128)(2,1)S(1)}, bf16[128,2048]{1,0:T(8,128)(2,1)}, u32[]{:S(2)}) copy-start(bf16[128,2048]{1,0:T(8,128)(2,1)} %param.7) | copy-start | bytes 1572868
  29.8 8.0 %copy-start.1 = (bf16[1,4,16,24,768]{4,3,2,1,0:T(8,128)(2,1)S(1)}, bf16[1,4,16,24,768]{4,3,2,1,0:T(8,128)(2,1)}, u32[]{:S(2)}) copy-start(bf16[1,4,16,24,768]{4,3,2,1,0:T(8,128)(2,1)} %param.11) | copy-start | bytes 7077892
  29.8 100.1 %all-to-all-start = ((bf16[4,16,24,2048]{3,2,0,1:T(8,128)(2,1)}), bf16[4,16,24,2048]{3,2,0,1:T(8,128)(2,1)}, u32[]{:S(2)}, u32[]{:S(2)}) async-start(bf16[4,16,24,2048]{3,2,0,1:T(8,128)(2,1)} %copy.47), calls=%async_computation | async-start | bytes 12582912 | tf_op jit(solution)/shard_map/all_to_all | solution.py:41
  39.0 95.7 %copy-start.8 = (bf16[1,1,16,24,768]{4,3,2,1,0:T(8,128)(2,1)S(1)}, bf16[1,1,16,24,768]{4,3,2,1,0:T(8,128)(2,1)}, u32[]{:S(2)}) copy-start(bf16[1,1,16,24,768]{4,3,2,1,0:T(8,128)(2,1)} %get-tuple-element.11) | copy-start | bytes 1769476
  129.9 11.9 %slice-start = ((s8[12582912]{0:T(1024)(128)(4,1)}), s8[4194304]{0:T(1024)(128)(4,1)S(1)}, s32[]{:S(2)}) async-start(s8[12582912]{0:T(1024)(128)(4,1)} %bitcast.111), calls=%async_computation.5 | async-start | bytes 8388608
  129.9 11.9 %slice-start.1 = ((s8[12582912]{0:T(1024)(128)(4,1)}), s8[4194304]{0:T(1024)(128)(4,1)S(1)}, s32[]{:S(2)}) async-start(s8[12582912]{0:T(1024)(128)(4,1)} %bitcast.111), calls=%async_computation.6 | async-start | bytes 8388608
  134.7 8.7 %copy-start.2 = (bf16[1,16,24,2048]{3,2,0,1:T(8,128)(2,1)}, bf16[1,16,24,2048]{3,2,0,1:T(8,128)(2,1)S(1)}, u32[]{:S(2)}) copy-start(bf16[1,16,24,2048]{3,2,0,1:T(8,128)(2,1)S(1)} %get-tuple-element.8) | copy-start | bytes 4718596
  134.7 13.7 %copy-start.4 = (bf16[1,16,24,2048]{3,2,0,1:T(8,128)(2,1)}, bf16[1,16,24,2048]{3,2,0,1:T(8,128)(2,1)S(1)}, u32[]{:S(2)}) copy-start(bf16[1,16,24,2048]{3,2,0,1:T(8,128)(2,1)S(1)} %get-tuple-element.6) | copy-start | bytes 4718596
  138.2 3.6 copy-start.7
  138.2 3.6 slice-start.2
  143.4 3.5 copy-start.6
  156.9 11.8 %all-to-all-start.1 = ((f32[4,16,24]{2,0,1:T(4,128)}), f32[4,16,24]{2,0,1:T(4,128)S(1)}, u32[]{:S(2)}, u32[]{:S(2)}) async-start(f32[4,16,24]{2,0,1:T(4,128)} %pad_maximum_fusion.2), calls=%async_computation.2 | async-start | bytes 65536 | tf_op jit(solution)/shard_map/all_to_all | solution.py:67
  162.3 194.6 %all-reduce.2.cloned.1.call-start = ((), (), s32[]{:S(2)}) async-start(), calls=%async_computation.4 | async-start | bytes 1048576 | tf_op jit(solution)/shard_map/psum | solution.py:80
  168.8 6.5 %copy-start.11 = (f32[128,8]{0,1:T(8,128)S(1)}, f32[128,8]{0,1:T(8,128)}, u32[]{:S(2)}) copy-start(f32[128,8]{0,1:T(8,128)} %param.9) | copy-start | bytes 12292
  168.8 6.5 %copy-start.10 = (s32[128,8]{0,1:T(8,128)S(1)}, s32[128,8]{0,1:T(8,128)}, u32[]{:S(2)}) copy-start(s32[128,8]{0,1:T(8,128)} %param.10) | copy-start | bytes 12292
  176.4 180.5 %reduce-scatter.2.cloned.1.call-start = ((), (), s32[]{:S(2)}) async-start(), calls=%async_computation.3 | async-start | bytes 14155776 | tf_op jit(solution)/shard_map/reduce_scatter | solution.py:62
  187.2 3.9 %copy-start.5 = (bf16[1,16,24,2048]{3,2,0,1:T(8,128)(2,1)S(1)}, bf16[1,16,24,2048]{3,2,0,1:T(8,128)(2,1)}, u32[]{:S(2)}) copy-start(bf16[1,16,24,2048]{3,2,0,1:T(8,128)(2,1)} %copy-done.4) | copy-start | bytes 4718596
  191.1 3.5 copy-start.3
  202.0 1.7 copy-start.9
Sparse Core Ops, SparseCore 0:
  176.5 180.2 all-reduce.1
Sparse Core Ops, SparseCore 1:
  187.3 75.3 reduce-scatter.1
where the time goes:
time: 367 us; the launch traced here: 366 us
  waiting for transfers between devices  244 us (66%)
  matrix products  43 us (12%)
  other arithmetic  27.2 us (7%)
  local copies, waits for them, and re-layouts  22.6 us (6%)
  between operations  15.8 us (4%)
  starting transfers between devices  13.5 us (4%)
    psum x1, waiting for transfers between devices, local(): router_grad = lax.psum(router_part, ('dp', 'expert'))  152 us
    all_to_all x1, waiting for transfers between devices, local(): lax.all_to_all(packed, 'expert', split_axis=1, concat_axis=1, tiled=True)  90.8 us
    dot_general x4, matrix products, local(): lax.dot_general(slot_rows, slot_acts, (((0,), (0,)), ((), ())), preferred...  15.5 us
    dot_general x4, matrix products, local(): jnp.dot(slot_rows, weight, preferred_element_type=jnp.float32)  14.8 us
    another operation x1, other arithmetic, local(): jnp.stack(weight_terms).astype(jnp.bfloat16)  10.7 us
    scatter x1, other arithmetic, pack_rows(): filled = zero_rows.at[flat_index.reshape(-1)].set(scaled.reshape(-1, width))  10.6 us
    dot_general x4, matrix products, local(): lax.dot_general(slot_acts, weight, (((1,), (1,)), ((), ())), preferred_el...  10.5 us
    all_to_all x1, starting transfers between devices, local(): lax.all_to_all(packed, 'expert', split_axis=1, concat_axis=1, tiled=True)  7.77 us
  transfers between devices with their start and end apart: 4, of which 3 were waited for; matrix products, arithmetic and copies ran while one was open for 9% of the time, Pallas kernels for 0%

commit v1 on v0

--- a/solution.py
+++ b/solution.py
@@ -2,6 +2,7 @@
 import jax.numpy as jnp
 from jax import lax
 from jax.sharding import PartitionSpec as P
+from jax.lax import all_gather
 
 
 def make_marks(block_routes, total_experts):
@@ -77,7 +78,7 @@
     router_part = lax.dot_general(
         dense_grad, inputs, (((0,), (0,)), ((), ())), preferred_element_type=jnp.float32
     )
-    router_grad = lax.psum(router_part, ("dp", "expert"))
+    router_grad = jnp.sum(all_gather(router_part, ("dp", "expert")), 0)
     return (hidden_grad, down_grad, input_grad, router_grad)
 
 

time: 367 us -> 406 us (1.11)
  waiting for transfers between devices: 244 us -> 269 us
  other arithmetic: 27.2 us -> 44.3 us
    all_gather x0 -> x1, waiting for transfers between devices: none -> 172 us  [local(): router_grad = jnp.sum(all_gather(router_part, ('dp', 'expert')), 0)]
    psum x1 -> x0, waiting for transfers between devices: 152 us -> none  [local(): router_grad = lax.psum(router_part, ('dp', 'expert'))]
    reduce_sum x0 -> x1, other arithmetic: none -> 21.7 us  [local(): router_grad = jnp.sum(all_gather(router_part, ('dp', 'expert')), 0)]
    dot_general x4, matrix products: 15.5 us -> 9.08 us  [local(): lax.dot_general(slot_rows, slot_acts, (((0,), (0,)), ((), ())), preferred...]
    all_to_all x1, waiting for transfers between devices: 1.26 us -> 6.39 us  [local(): lax.all_to_all(slot_products, 'expert', split_axis=1, concat_axis=1, tile...]
    another operation x1, other arithmetic: 10.7 us -> 6.09 us  [local(): jnp.stack(weight_terms).astype(jnp.bfloat16)]
    dot_general x4, matrix products: 10.5 us -> 14.8 us  [local(): lax.dot_general(slot_acts, weight, (((1,), (1,)), ((), ())), preferred_el...]
  transfers between devices with their start and end apart: 4 -> 4, of which waited for: 3 -> 3; matrix products, arithmetic and copies ran while one was open for 9% -> 14% of each run, Pallas kernels for 0% -> 0%
where the time goes in v1:
time: 406 us
  waiting for transfers between devices  269 us (66%)
  other arithmetic  44.3 us (11%)
  matrix products  40.4 us (10%)
  local copies, waits for them, and re-layouts  22.5 us (6%)
  between operations  15.8 us (4%)
  starting transfers between devices  13.5 us (3%)
    all_gather x1, waiting for transfers between devices, local(): router_grad = jnp.sum(all_gather(router_part, ('dp', 'expert')), 0)  172 us
    all_to_all x1, waiting for transfers between devices, local(): lax.all_to_all(packed, 'expert', split_axis=1, concat_axis=1, tiled=True)  90.8 us
    reduce_sum x1, other arithmetic, local(): router_grad = jnp.sum(all_gather(router_part, ('dp', 'expert')), 0)  21.7 us
    dot_general x4, matrix products, local(): lax.dot_general(slot_acts, weight, (((1,), (1,)), ((), ())), preferred_el...  14.8 us
    dot_general x4, matrix products, local(): jnp.dot(slot_rows, weight, preferred_element_type=jnp.float32)  14.2 us
    scatter x1, other arithmetic, pack_rows(): filled = zero_rows.at[flat_index.reshape(-1)].set(scaled.reshape(-1, width))  10.6 us
    dot_general x4, matrix products, local(): lax.dot_general(slot_rows, slot_acts, (((0,), (0,)), ((), ())), preferred...  9.08 us
  transfers between devices with their start and end apart: 4, of which 3 were waited for; matrix products, arithmetic and copies ran while one was open for 14% of the time, Pallas kernels for 0%

profile of v1, /device:TPU:1, one launch (start us, length us, event | category | flops | bytes accessed | tf_op | source)
XLA Modules:
  0.0 405.7 jit_solution(11098932272805189669)
XLA Ops:
  8.0 0.8 fusion.55
  8.9 0.7 select_reduce_fusion.1
  10.6 1.1 convert_element_type.50
  11.7 0.8 copy.46
  12.6 10.6 %scatter_custom_fusion = bf16[1536,2048]{1,0:T(8,128)(2,1)} fusion(s32[1024]{0:T(1024)S(1)} %bitcast.110, f32[128,2048]{1,0:T(8,128)S(1)} %convert_element_type.50, f32[1024]{0:T(1024)S(1)} %mul.48, bf16[]{:T(256)} %constant.31.clone.1), kind=kCustom, calls=%fused_computation.5 | custom fusion | flops 4194304 | bytes 7344130 | tf_op jit(solution)/shard_map/scatter | solution.py:25
  23.2 6.6 %copy.47 = bf16[4,16,24,2048]{3,2,0,1:T(8,128)(2,1)} copy(bf16[4,16,24,2048]{3,2,1,0:T(8,128)(2,1)} %bitcast.85) | data formatting | bytes 12582912 | tf_op jit(solution)/shard_map/reshape | solution.py:26
  29.8 7.8 %all-to-all-start = ((bf16[4,16,24,2048]{3,2,0,1:T(8,128)(2,1)}), bf16[4,16,24,2048]{3,2,0,1:T(8,128)(2,1)}, u32[]{:S(2)}, u32[]{:S(2)}) async-start(bf16[4,16,24,2048]{3,2,0,1:T(8,128)(2,1)} %copy.47), calls=%async_computation | async-start | bytes 12582912 | tf_op jit(solution)/shard_map/all_to_all | solution.py:42
  37.8 1.2 fusion.70
  39.0 90.8 %all-to-all-done = bf16[4,16,24,2048]{3,2,0,1:T(8,128)(2,1)} async-done(((bf16[4,16,24,2048]{3,2,0,1:T(8,128)(2,1)}), bf16[4,16,24,2048]{3,2,0,1:T(8,128)(2,1)}, u32[]{:S(2)}, u32[]{:S(2)}) %all-to-all-start) | async-done | bytes 6291488 | tf_op jit(solution)/shard_map/all_to_all | solution.py:42
  129.9 5.4 %fusion.69 = (bf16[1,16,24,2048]{3,2,0,1:T(8,128)(2,1)S(1)}, bf16[1,16,24,2048]{3,2,0,1:T(8,128)(2,1)S(1)}, bf16[1,16,24,2048]{3,2,0,1:T(8,128)(2,1)}, bf16[1,16,24,2048]{3,2,0,1:T(8,128)(2,1)}) fusion(bf16[4,16,24,2048]{3,2,0,1:T(8,128)(2,1)} %all-to-all-done), kind=kLoop, calls=%fused_computation.80 | loop fusion | bytes 12582912 | tf_op jit(solution)/shard_map/slice | solution.py:48
  135.3 1.1 copy-done.7
  136.5 3.4 multiply_reduce_fusion
  140.0 4.1 %multiply_reduce_fusion.1 = f32[384]{0:T(512)S(1)} fusion(bf16[384,2048]{1,0:T(8,128)(2,1)} %bitcast.92, bf16[384,768]{1,0:T(8,128)(2,1)} %bitcast.102, bf16[4,2048,768]{2,1,0:T(8,128)(2,1)} %param.12), kind=kOutput, calls=%fused_computation.29 | convolution fusion | flops 1210318464 | bytes 5309952 | tf_op jit(solution)/shard_map/dot_general | solution.py:51
  144.2 3.9 multiply_reduce_fusion.2
  148.2 3.4 multiply_reduce_fusion.3
  152.3 5.4 %all-to-all-start.1 = ((f32[4,16,24]{2,0,1:T(4,128)}), f32[4,16,24]{2,0,1:T(4,128)S(1)}, u32[]{:S(2)}, u32[]{:S(2)}) async-start(f32[4,16,24]{2,0,1:T(4,128)} %pad_maximum_fusion.2), calls=%async_computation.2 | async-start | bytes 65536 | tf_op jit(solution)/shard_map/all_to_all | solution.py:68
  157.8 6.4 %all-to-all-done.1 = f32[4,16,24]{2,0,1:T(4,128)S(1)} async-done(((f32[4,16,24]{2,0,1:T(4,128)}), f32[4,16,24]{2,0,1:T(4,128)S(1)}, u32[]{:S(2)}, u32[]{:S(2)}) %all-to-all-start.1) | async-done | bytes 6176 | tf_op jit(solution)/shard_map/all_to_all | solution.py:68
  164.3 6.2 %gather_fusion = f32[1024]{0:T(1024)S(1)} fusion(f32[1536]{0:T(1024)S(1)} %reshape.84, s32[1024]{0:T(1024)S(1)} %broadcast_clamp_fusion), kind=kCustom, calls=%fused_computation | custom fusion | bytes 12288 | tf_op jit(solution)/shard_map/gather | solution.py:70
  170.8 1.0 fusion.71
  172.2 3.5 fusion.25
  175.7 1.8 fusion.24
  177.6 1.9 fusion.23
  179.4 1.9 fusion.22
  181.3 6.1 %pad_maximum_fusion = bf16[4,2048,768]{2,1,0:T(8,128)(2,1)} fusion(bf16[1,2048,768]{2,1,0:T(8,128)(2,1)S(1)} %fusion.25, bf16[1,2048,768]{2,1,0:T(8,128)(2,1)S(1)} %fusion.24, bf16[1,2048,768]{2,1,0:T(8,128)(2,1)S(1)} %fusion.23, bf16[1,2048,768]{2,1,0:T(8,128)(2,1)S(1)} %fusion.22), kind=kLoop, calls=%fused_computation.2 | loop fusion | flops 18874368 | bytes 25165824 | tf_op jit(solution)/shard_map/stack | solution.py:64
  187.4 3.9 fusion.51
  191.3 3.4 fusion.48
  194.8 3.3 fusion.45
  198.1 3.6 fusion.42
  201.7 1.7 pad_maximum_fusion.1
  203.4 1.1 convolution_convert_fusion.4
  204.5 172.0 %all-gather.3.cloned.1.call-done = f32[8192,2048]{1,0:T(8,128)} async-done(((f32[64,2048]{1,0:T(8,128)}), f32[8192,2048]{1,0:T(8,128)}) %all-gather.3.cloned.1.call-update) | async-done | bytes 67108880 | tf_op jit(solution)/shard_map/all_gather | solution.py:81
  376.6 21.7 %reduce_sum.92 = f32[64,2048]{1,0:T(8,128)} reduce(f32[128,64,2048]{2,1,0:T(8,128)} %bitcast.23, f32[]{:T(128)} %constant.40.clone.1), dimensions={0}, to_apply=%region_10.11 | reduce | flops 16646144 | bytes 67633152 | tf_op jit(solution)/shard_map/reduce_sum | solution.py:81
  (53 shorter events, 3.2 us)
Async XLA Ops:
  8.0 162.8 %copy-start = (bf16[128,2048]{1,0:T(8,128)(2,1)S(1)}, bf16[128,2048]{1,0:T(8,128)(2,1)}, u32[]{:S(2)}) copy-start(bf16[128,2048]{1,0:T(8,128)(2,1)} %param.7) | copy-start | bytes 1572868
  29.8 8.0 %copy-start.2 = (bf16[1,4,16,24,768]{4,3,2,1,0:T(8,128)(2,1)S(1)}, bf16[1,4,16,24,768]{4,3,2,1,0:T(8,128)(2,1)}, u32[]{:S(2)}) copy-start(bf16[1,4,16,24,768]{4,3,2,1,0:T(8,128)(2,1)} %param.11) | copy-start | bytes 7077892
  29.8 100.1 %all-to-all-start = ((bf16[4,16,24,2048]{3,2,0,1:T(8,128)(2,1)}), bf16[4,16,24,2048]{3,2,0,1:T(8,128)(2,1)}, u32[]{:S(2)}, u32[]{:S(2)}) async-start(bf16[4,16,24,2048]{3,2,0,1:T(8,128)(2,1)} %copy.47), calls=%async_computation | async-start | bytes 12582912 | tf_op jit(solution)/shard_map/all_to_all | solution.py:42
  39.0 97.4 %copy-start.10 = (bf16[1,1,16,24,768]{4,3,2,1,0:T(8,128)(2,1)S(1)}, bf16[1,1,16,24,768]{4,3,2,1,0:T(8,128)(2,1)}, u32[]{:S(2)}) copy-start(bf16[1,1,16,24,768]{4,3,2,1,0:T(8,128)(2,1)} %get-tuple-element.12) | copy-start | bytes 1769476
  135.3 1.1 copy-start.7
  140.0 4.2 %copy-start.8 = (bf16[1,1,16,24,768]{4,3,2,1,0:T(8,128)(2,1)S(1)}, bf16[1,1,16,24,768]{4,3,2,1,0:T(8,128)(2,1)}, u32[]{:S(2)}) copy-start(bf16[1,1,16,24,768]{4,3,2,1,0:T(8,128)(2,1)} %get-tuple-element.11) | copy-start | bytes 1769476
  152.3 11.8 %all-to-all-start.1 = ((f32[4,16,24]{2,0,1:T(4,128)}), f32[4,16,24]{2,0,1:T(4,128)S(1)}, u32[]{:S(2)}, u32[]{:S(2)}) async-start(f32[4,16,24]{2,0,1:T(4,128)} %pad_maximum_fusion.2), calls=%async_computation.2 | async-start | bytes 65536 | tf_op jit(solution)/shard_map/all_to_all | solution.py:68
  157.7 218.8 %all-gather.3.cloned.1.call-start = ((), (), s32[]{:S(2)}) async-start(), calls=%async_computation.4 | async-start | bytes 67633152 | tf_op jit(solution)/shard_map/all_gather | solution.py:81
  164.3 6.5 %copy-start.13 = (f32[128,8]{0,1:T(8,128)S(1)}, f32[128,8]{0,1:T(8,128)}, u32[]{:S(2)}) copy-start(f32[128,8]{0,1:T(8,128)} %param.9) | copy-start | bytes 12292
  164.3 6.5 %copy-start.12 = (s32[128,8]{0,1:T(8,128)S(1)}, s32[128,8]{0,1:T(8,128)}, u32[]{:S(2)}) copy-start(s32[128,8]{0,1:T(8,128)} %param.10) | copy-start | bytes 12292
  171.9 226.4 %reduce-scatter.2.cloned.1.call-start = ((), (), s32[]{:S(2)}) async-start(), calls=%async_computation.3 | async-start | bytes 14155776 | tf_op jit(solution)/shard_map/reduce_scatter | solution.py:63
  172.1 3.6 copy-start.5
  172.1 3.5 copy-start.9
  175.7 1.9 copy-start.3
  187.4 3.9 copy-start.6
  191.3 3.4 copy-start.4
  201.7 1.7 copy-start.11
  376.6 21.7 %copy-start.1 = (bf16[128,2048]{1,0:T(8,128)(2,1)S(1)}, bf16[128,2048]{1,0:T(8,128)(2,1)}, u32[]{:S(2)}) copy-start(bf16[128,2048]{1,0:T(8,128)(2,1)} %param.7) | copy-start | bytes 1572868
Sparse Core Ops, SparseCore 0:
  172.0 204.5 all-gather.2
Sparse Core Ops, SparseCore 1:
  187.5 168.0 reduce-scatter.1
